TPU v7x, 512 devices: a whole 4x4x16 slice. The times are simulated.
512 devices in a mesh: dp: 64 (over x_lo, z, core), ctx: 8 (over x_hi, y).
Axes of the slice: x: 4 (x_hi: 2, x_lo: 2; x = x_hi * 2 + x_lo), y: 4, z: 16, core: 2. Of those that a mesh axis runs over, the one named last changes fastest.
Arguments:
- query_vecs: bfloat16 [64, 1024, 1024], P('dp', 'ctx'), may hold values from -12 to 12, as said below
- key_vecs: bfloat16 [64, 1024, 1024], P('dp', 'ctx'), may hold values from -12 to 12
- value_vecs: bfloat16 [64, 1024, 1024], P('dp', 'ctx'), may hold values from -6 to 6
- residual: bfloat16 [64, 1024, 2048], P('dp', 'ctx'), may hold values from -45 to 45
- w_out: bfloat16 [1024, 2048], P('dp'), may hold values from -0.75 to 0.75
- norm_gain: float32 [2048], replicated, may hold values from 0.25 to 1.75
- w_gate_up: bfloat16 [64, 2, 2048, 1408], P('dp', None, None, 'ctx'), may hold values from -0.125 to 0.125
- w_down: bfloat16 [64, 1408, 2048], P('dp', 'ctx'), may hold values from -0.15625 to 0.15625
- expert_ids: int32 [64, 1024, 6], P('dp', 'ctx'), may hold values from 0 to 63, as said below
- route_gates: float32 [64, 1024, 6], P('dp', 'ctx'), may hold values from 0.1 to 0.9
- capacity: int32 [64, 8, 2], P('dp', 'ctx'), may hold values from 12 to 24, as said below
- expert_owner: int32 [64], replicated, may hold values from 0 to 63, each once
Outputs:
- attn_proj: bfloat16 [64, 1024, 2048], P('dp', 'ctx')
- expert_sum: bfloat16 [64, 1024, 2048], P('dp', 'ctx')
Inputs may be any that keep to these rules, and one draw needn't show every extreme that they name: `query_vecs`: q and k are drawn together. `expert_ids`: each position names 6 different experts; in each aligned block of 128 positions, experts 0 to 1 are each named by at least 24 positions. In each block some expert has capacity 24. `expert_owner`: each index of dp holds one expert.
All inputs are finite; a program needn't handle non-finite values.
Results may differ from a plain program's by a relative error of at most 0.019.
Values may be sent and summed in bfloat16 or wider, within the bound.
A program may use at most 64 MiB of HBM per device.

v0:
```python
import jax
import jax.numpy as jnp
from jax import lax
from jax.sharding import PartitionSpec as P

HEADS = 8
HD = 128
PASS_SPECIALISTS = 2
CAP = 24


EPSILON = 1e-06
LOWEST = -1e30


def broadcast(array, axis, root):
    mine = lax.axis_index(axis) == root
    return lax.psum(jnp.where(mine, array, jnp.zeros_like(array)), axis)


def route_slots(expert_ids, route_gates, capacity, expert):
    matches = expert_ids == expert
    routed = jnp.any(matches, axis=1)
    gate_value = jnp.sum(jnp.where(matches, route_gates, 0.0), axis=1)
    slot_rank = jnp.cumsum(routed.astype(jnp.int32)) - 1
    kept_mask = routed & (slot_rank < capacity[expert])
    return (slot_rank, kept_mask, gate_value)


def softmax_block(running, pieces, queries, first_row):
    top_seen, denominator, weighted = running
    key_block = pieces[0][0]
    value_block = pieces[1][0]
    width = key_block.shape[0]
    token_count = queries.shape[0]
    key_heads = key_block.reshape(width, HEADS, HD)
    value_heads = value_block.reshape(width, HEADS, HD)
    gating_logits = jnp.einsum(
        "qhd,khd->qhk", queries, key_heads, preferred_element_type=jnp.float32
    ) * HD ** (-0.5)
    query_pos = first_row + jnp.arange(token_count)
    key_pos = jnp.arange(width)
    visible = key_pos[None, :] <= query_pos[:, None]
    gating_logits = jnp.where(visible[:, None, :], gating_logits, -jnp.inf)
    newest = jnp.maximum(top_seen, jnp.max(gating_logits, axis=-1))
    weights = jnp.exp(gating_logits - newest[:, :, None])
    denominator = jnp.sum(weights, axis=-1)
    weighted = jnp.einsum(
        "qhk,khd->qhd",
        weights.astype(jnp.bfloat16),
        value_heads,
        preferred_element_type=jnp.float32,
    )
    return (newest, denominator, weighted)


def body(
    query_vecs,
    key_vecs,
    value_vecs,
    residual,
    w_out,
    norm_gain,
    w_gate_up,
    w_down,
    expert_ids,
    route_gates,
    capacity,
    expert_owner,
):
    token_count = query_vecs.shape[1]
    weights_in = []
    for expert in range(PASS_SPECIALISTS):
        weights_in.append(
            (
                broadcast(w_gate_up[0], "dp", expert_owner[expert]),
                broadcast(w_down[0], "dp", expert_owner[expert]),
            )
        )
    queries = query_vecs[0].reshape(token_count, HEADS, HD)
    first_row = lax.axis_index("ctx") * token_count
    start_state = (
        jnp.full((token_count, HEADS), LOWEST, jnp.float32),
        jnp.zeros((token_count, HEADS), jnp.float32),
        jnp.zeros((token_count, HEADS, HD), jnp.float32),
    )
    top_seen, denominator, weighted = softmax_block(
        start_state,
        (
            lax.all_gather(key_vecs, "ctx", axis=1, tiled=True),
            lax.all_gather(value_vecs, "ctx", axis=1, tiled=True),
        ),
        queries,
        first_row,
    )
    attended = (
        (weighted / denominator[:, :, None]).astype(jnp.bfloat16).reshape(token_count, HEADS * HD)
    )
    projected = jnp.dot(
        attended,
        lax.all_gather(w_out, "dp", axis=0, tiled=True),
        preferred_element_type=jnp.float32,
    )
    attn_proj = projected.astype(jnp.bfloat16)
    combined = residual[0].astype(jnp.float32) + attn_proj.astype(jnp.float32)
    normed = (
        combined
        * lax.rsqrt(jnp.mean(combined * combined, axis=-1, keepdims=True) + EPSILON)
        * norm_gain
    ).astype(jnp.bfloat16)
    block_caps = capacity[0, 0]
    slot_ids = jnp.arange(CAP)
    dispatched = []
    routing = []
    for expert in range(PASS_SPECIALISTS):
        slot_rank, kept_mask, gate_value = route_slots(
            expert_ids[0], route_gates[0], block_caps, expert
        )
        select = ((slot_rank[None, :] == slot_ids[:, None]) & kept_mask[None, :]).astype(
            jnp.bfloat16
        )
        dispatched.append(
            jnp.dot(select, normed, preferred_element_type=jnp.float32).astype(jnp.bfloat16)
        )
        routing.append((slot_rank, kept_mask, gate_value))
    routed_rows = lax.all_gather(jnp.stack(dispatched, axis=1), "ctx", axis=0, tiled=True)
    outputs = []
    for expert_expert in range(PASS_SPECIALISTS):
        gate_up, down_part = weights_in[expert_expert]
        source = routed_rows[:, expert_expert]
        gate_proj = jnp.dot(source, gate_up[0], preferred_element_type=jnp.float32)
        up_proj = jnp.dot(source, gate_up[1], preferred_element_type=jnp.float32)
        hidden = (jax.nn.silu(gate_proj) * up_proj).astype(jnp.bfloat16)
        outputs.append(jnp.dot(hidden, down_part, preferred_element_type=jnp.float32))
    expert_out = lax.psum_scatter(
        jnp.stack(outputs, axis=1).astype(jnp.bfloat16), "ctx", scatter_dimension=0, tiled=True
    ).astype(jnp.float32)
    summed = jnp.zeros((token_count, normed.shape[1]), jnp.float32)
    for expert in range(PASS_SPECIALISTS):
        slot_rank, kept_mask, gate_value = routing[expert]
        picked = jnp.take(expert_out[:, expert], jnp.clip(slot_rank, 0, CAP - 1), axis=0)
        summed = summed + jnp.where(kept_mask, gate_value, 0.0)[:, None] * picked
    expert_sum = summed.astype(jnp.bfloat16)
    return (attn_proj[None], expert_sum[None])


def solution(mesh):
    placed = (
        P("dp", "ctx", None),
        P("dp", "ctx", None),
        P("dp", "ctx", None),
        P("dp", "ctx", None),
        P("dp", None),
        P(),
        P("dp", None, None, "ctx"),
        P("dp", "ctx", None),
        P("dp", "ctx", None),
        P("dp", "ctx", None),
        P("dp", "ctx", None),
        P(),
    )
    return jax.shard_map(
        body,
        mesh=mesh,
        in_specs=placed,
        out_specs=(P("dp", "ctx", None), P("dp", "ctx", None)),
        check_vma=False,
    )
```

profile of v0, /device:TPU:25, one launch (start us, length us, event | category | flops | bytes accessed | tf_op | source)
XLA Modules:
  0.0 889.2 jit_solution(2206888241742193926)
XLA Ops:
  8.0 1.8 copy.26
  10.6 1.4 fusion.58
  13.3 2.3 select_bitcast_fusion.3
  15.6 1.9 select_bitcast_fusion.1
  19.9 1.2 broadcast_select_fusion
  21.1 1.2 broadcast_select_fusion.1
  22.4 60.1 %all-gather.7.cloned.1.call-done = bf16[1,1024,1024]{2,1,0:T(8,128)(2,1)} async-done(((bf16[1,128,1024]{2,1,0:T(8,128)(2,1)}), bf16[1,1024,1024]{2,1,0:T(8,128)(2,1)}) %all-gather.7.cloned.1.call-update) | async-done | bytes 2097168 | tf_op jit(solution)/shard_map/all_gather | solution.py:91
  82.5 2.9 copy.29
  85.3 68.5 %all-gather.5.cloned.1.call-done = bf16[1,1024,1024]{1,2,0:T(8,128)(2,1)} async-done(((bf16[1,128,1024]{1,2,0:T(8,128)(2,1)}), bf16[1,1024,1024]{1,2,0:T(8,128)(2,1)}) %all-gather.5.cloned.1.call-update) | async-done | bytes 2097168 | tf_op jit(solution)/shard_map/all_gather | solution.py:90
  153.9 2.7 fusion.2
  157.5 1.5 fusion.23
  159.0 122.3 %all-gather.9.cloned.1.call-done = bf16[1024,2048]{1,0:T(8,128)(2,1)} async-done(((bf16[16,2048]{1,0:T(8,128)(2,1)}), bf16[1024,2048]{1,0:T(8,128)(2,1)}) %all-gather.9.cloned.1.call-update) | async-done | bytes 4194320 | tf_op jit(solution)/shard_map/all_gather | solution.py:101
  281.3 3.0 multiply_reduce_fusion
  285.8 433.3 %all-reduce.3.cloned.1.call-done = (bf16[176,2048]{1,0:T(8,128)(2,1)}, bf16[2,2048,176]{1,2,0:T(8,128)(2,1)}, bf16[176,2048]{1,0:T(8,128)(2,1)}, bf16[2,2048,176]{1,2,0:T(8,128)(2,1)}) async-done(((bf16[176,2048]{1,0:T(8,128)(2,1)}, bf16[2,2048,176]{1,2,0:T(8,128)(2,1)}, bf16[176,2048]{1,0:T(8,128)(2,1)}, bf16[2,2048,176]{1,2,0:T(8,128)(2,1)}), (bf16[176,2048]{1,0:T(8,128)(2,1)}, ...) | async-done | bytes 4325392 | tf_op jit(solution)/shard_map/psum | solution.py:18
  719.1 61.2 %all-gather.11.cloned.1.call-done = bf16[192,2,2048]{2,0,1:T(8,128)(2,1)} async-done(((bf16[24,2,2048]{2,0,1:T(8,128)(2,1)}), bf16[192,2,2048]{2,0,1:T(8,128)(2,1)}) %all-gather.11.cloned.1.call-update) | async-done | bytes 1572880 | tf_op jit(solution)/shard_map/all_gather | solution.py:126
  780.3 1.9 fusion.26
  782.2 1.5 fusion.27
  783.7 2.2 fusion.4
  786.0 2.5 fusion.3
  788.6 1.2 copy.38
  790.0 88.3 %reduce-scatter.4.cloned.1.call-done = bf16[24,4096]{1,0:T(8,128)(2,1)} async-done(((bf16[192,4096]{1,0:T(8,128)(2,1)}), bf16[24,4096]{1,0:T(8,128)(2,1)}) %reduce-scatter.4.cloned.1.call-update) | async-done | bytes 196624
  879.3 1.0 gather_fusion.1
  880.2 1.0 gather_fusion
  881.2 1.1 fusion.28
  (62 shorter events, 7.5 us)
Async XLA Ops:
  7.2 8.4 copy-start
  7.2 75.3 %all-gather.7.cloned.1.call-start = ((), (), s32[]{:S(2)}) async-start(), calls=%async_computation.2 | async-start | bytes 2359296 | tf_op jit(solution)/shard_map/all_gather | solution.py:91
  7.9 146.0 %all-gather.5.cloned.1.call-start = ((), (), s32[]{:S(2)}) async-start(), calls=%async_computation.1 | async-start | bytes 2359296 | tf_op jit(solution)/shard_map/all_gather | solution.py:90
  9.8 271.6 %all-gather.9.cloned.1.call-start = ((), (), s32[]{:S(2)}) async-start(), calls=%async_computation.3 | async-start | bytes 4259840 | tf_op jit(solution)/shard_map/all_gather | solution.py:101
  10.5 708.6 %all-reduce.3.cloned.1.call-start = ((), (), s32[]{:S(2)}) async-start(), calls=%async_computation.6 | async-start | bytes 8650752 | tf_op jit(solution)/shard_map/psum | solution.py:18
  17.4 0.9 copy-start.3
  17.4 1.0 copy-start.4
  17.4 1.6 copy-start.6
  17.4 2.2 copy-start.5
  17.5 762.8 %all-gather.11.cloned.1.call-start = ((), (), s32[]{:S(2)}) async-start(), calls=%async_computation.4 | async-start | bytes 1769472 | tf_op jit(solution)/shard_map/all_gather | solution.py:126
  157.5 123.9 %copy-start.1 = (bf16[1,128,2048]{2,1,0:T(8,128)(2,1)S(1)}, bf16[1,128,2048]{2,1,0:T(8,128)(2,1)}, u32[]{:S(2)}) copy-start(bf16[1,128,2048]{2,1,0:T(8,128)(2,1)} %param.17) | copy-start | bytes 1572868
  281.3 3.1 copy-start.7
  281.3 3.1 copy-start.11
  281.3 3.4 copy-start.8
  284.4 497.8 %copy-start.2 = (bf16[128,2048]{1,0:T(8,128)(2,1)}, bf16[128,2048]{1,0:T(8,128)(2,1)S(1)}, u32[]{:S(2)}) copy-start(bf16[128,2048]{1,0:T(8,128)(2,1)S(1)} %get-tuple-element.32) | copy-start | bytes 1572868
  285.8 592.5 %reduce-scatter.4.cloned.1.call-start = ((), (), s32[]{:S(2)}) async-start(), calls=%async_computation.5 | async-start | bytes 1769472
  780.3 1.9 copy-start.9
  780.3 3.4 copy-start.10
Sparse Core Ops, SparseCore 0:
  11.2 71.1 all-gather.6
  86.1 67.7 all-gather.4
  156.0 125.2 all-gather.8
  284.4 434.6 all-reduce.2
  722.7 57.5 all-gather.10
  790.0 88.2 reduce-scatter.3
where the time goes:
time: 891 us; the launch traced here: 889 us
  waiting for transfers between devices  835 us (94%)
  matrix products  16 us (2%)
  between operations  15.7 us (2%)
  local copies, waits for them, and re-layouts  11.1 us (1%)
  other arithmetic  11.1 us (1%)
    psum x1, waiting for transfers between devices, broadcast(): return lax.psum(jnp.where(mine, array, jnp.zeros_like(array)), axis)  433 us
    all_gather x1, waiting for transfers between devices, body(): lax.all_gather(w_out, 'dp', axis=0, tiled=True)  122 us
    unnamed x7, waiting for transfers between devices  89.7 us
    all_gather x1, waiting for transfers between devices, body(): lax.all_gather(key_vecs, 'ctx', axis=1, tiled=True)  68.5 us
    all_gather x1, waiting for transfers between devices, body(): lax.all_gather(jnp.stack(dispatched, axis=1), 'ctx', axis=0, tiled=True)  61.2 us
    all_gather x1, waiting for transfers between devices, body(): lax.all_gather(value_vecs, 'ctx', axis=1, tiled=True)  60.1 us
  transfers between devices with their start and end apart: 6, of which 6 were waited for; matrix products, arithmetic and copies ran while one was open for 3% of the time, Pallas kernels for 0%

commit v1 on v0

v1 whole, which is shorter than its diff:
```python
import functools

import jax
import jax.numpy as jnp
from jax import lax
from jax.experimental import pallas as pl
from jax.experimental.pallas import tpu as pltpu
from jax.sharding import PartitionSpec as P

D = 2048
HD = 128
FF_DEV = 176
CAP = 24
TOK = 128
NZ = 16
NY = 4
NX = 4
NCTX = 8
HALF = 272
HALF_STEP = 256
EPSILON = 1e-06
MESH = pl.DeviceIdType.MESH
BF = jnp.bfloat16
F32 = jnp.float32

NT = (((1,), (1,)), ((), ()))
TN = (((0,), (0,)), ((), ()))


def dot(a, b, dims=(((1,), (0,)), ((), ()))):
    return lax.dot_general(a, b, dims, preferred_element_type=F32)


def kernel(
    owner, caps,
    q_ref, k_ref, v_ref, res_ref, wo_ref, w_ref, gain_ref, ids_ref, gates_ref,
    proj_ref, sum_ref,
    qkv, abuf, attd, wbuf, res, own, oth, cand, rsb, xpiece, wf, uw,
    normed, rbuf, dsend, sbuf, pbuf, xo, xi,
    q_s, q_r, a_s, a_r, z_s, z_r, p1_s, p1_r, p2_s, p2_r, c_s, c_r,
    l_s, oth_s, oth_r, rs_s, rs_r, xp_s, xp_r, ag_s, ag_r, cc_s, cc_r,
    d_s, d_r, r_s, r_r, e_s, e_r, o_s, o_r,
):
    dp = lax.axis_index("dp")
    ctx = lax.axis_index("ctx")
    core = lax.rem(dp, 2)
    z = lax.rem(dp // 2, NZ)
    xl = dp // (2 * NZ)
    xh = ctx // NY
    y = lax.rem(ctx, NY)
    x = xh * 2 + xl

    def at(xx=None, yy=None, zz=None, cc=None):
        xx = x if xx is None else xx
        yy = y if yy is None else yy
        zz = z if zz is None else zz
        cc = core if cc is None else cc
        return ((lax.rem(xx, 2) * NZ + zz) * 2 + cc, (xx // 2) * NY + yy)

    partner = at(xx=x + 1 - 2 * xl)
    sibling = at(cc=1 - core)
    up = at(zz=lax.rem(z + 1, NZ))
    down = at(zz=lax.rem(z + NZ - 1, NZ))

    pending = []

    def send(src, dst, ssem, rsem, dev):
        copy = pltpu.make_async_remote_copy(
            src_ref=src, dst_ref=dst, send_sem=ssem, recv_sem=rsem,
            device_id=dev, device_id_type=MESH,
        )
        copy.start()
        pending.append(copy)

    def arrive(dst, sem):
        pltpu.make_async_copy(dst, dst, sem).wait()

    barrier = pltpu.get_barrier_semaphore()
    partners = [at(zz=lax.rem(z + i, NZ)) for i in range(1, NZ)]
    partners += [(dp, lax.rem(ctx + i, NCTX)) for i in range(1, NCTX)]
    partners += [partner, at(xx=lax.rem(x + 3 - 2 * xl, NX)), sibling]
    for dev in partners:
        pl.semaphore_signal(barrier, inc=1, device_id=dev, device_id_type=MESH)
    pl.semaphore_wait(barrier, len(partners))

    def cols(start, size):
        return pl.ds(pl.multiple_of(start, 128), size)

    half_rows = pl.ds(pl.multiple_of(core * HALF_STEP, 16), HALF)
    other_rows = pl.ds(pl.multiple_of((1 - core) * HALF_STEP, 16), HALF)
    send(w_ref.at[other_rows, :], oth, oth_s, oth_r, sibling)
    own_copy = pltpu.make_async_copy(w_ref.at[half_rows, :], own, l_s.at[0])
    own_copy.start()
    for i in range(1, NCTX):
        peer = lax.rem(ctx + i, NCTX)
        for j, ref in enumerate((q_ref, k_ref, v_ref)):
            send(ref.at[:, cols(peer * HD, HD)], qkv.at[j, ctx], q_s.at[j, i], q_r.at[j, ctx], (dp, peer))
    for j, ref in enumerate((q_ref, k_ref, v_ref)):
        pltpu.make_async_copy(ref.at[:, cols(ctx * HD, HD)], qkv.at[j, ctx], q_r.at[j, ctx]).start()
    for i in range(1, NZ):
        send(wo_ref.at[:, cols(ctx * 256, 256)], wbuf.at[x, y, z, core], z_s.at[i], z_r.at[z], at(zz=lax.rem(z + i, NZ)))
    pltpu.make_async_copy(wo_ref.at[:, cols(ctx * 256, 256)], wbuf.at[x, y, z, core], z_r.at[z]).start()
    res_copy = pltpu.make_async_copy(res_ref, res, l_s.at[1])
    res_copy.start()

    owner0 = owner[0]
    owner1 = owner[1]

    def weights():
        own_copy.wait()
        arrive(oth, oth_r)
        mate = dp + 1 - 2 * core
        has = []
        for e, root in enumerate((owner0, owner1)):
            mine = root == dp
            mates = root == mate
            has.append(jnp.logical_or(mine, mates))
            for c in range(NZ):
                a = own[:, c * 128:(c + 1) * 128]
                b = oth[:, c * 128:(c + 1) * 128]
                cand[e, c] = lax.select(mine, a, lax.select(mates, b, jnp.zeros_like(b)))
        to = (up, down)

        def chunk(d, t):
            return lax.rem(z + 2 * NZ - 2 - t, NZ) if d == 0 else lax.rem(z + 2 + t, NZ)

        for d in range(2):
            send(cand.at[d, chunk(d, -1)], rsb.at[d, 0], rs_s.at[d, 0], rs_r.at[d, 0], to[d])
        yield
        for t in range(NZ - 1):
            for d in range(2):
                arrive(rsb.at[d, t], rs_r.at[d, t])
                rsb[d, t] = lax.select(has[d], cand[d, chunk(d, t)], rsb[d, t])
                if t < NZ - 2:
                    send(rsb.at[d, t], rsb.at[d, t + 1], rs_s.at[d, t + 1], rs_r.at[d, t + 1], to[d])
            yield
        send(rsb.at[1 - xl, NZ - 2], xpiece, xp_s, xp_r, partner)
        yield
        arrive(xpiece, xp_r)
        root = jnp.where(xl == 0, owner0, owner1)
        there = (root // (2 * NZ)) != xl
        wf[core, :, cols(z * 128, 128)] = lax.select(there, xpiece[...], rsb[xl, NZ - 2])

        def piece(c):
            return wf.at[core, :, cols(c * 128, 128)]

        for d in range(2):
            send(piece(z), piece(z), ag_s.at[d, 0], ag_r.at[d, 0], to[d])
        send(piece(z), piece(z), cc_s.at[0], cc_r.at[z], sibling)
        yield
        for t in range(NZ // 2):
            for d in range(2):
                last = NZ // 2 - 1 - d
                if t > last:
                    continue
                c = lax.rem(z + NZ - 1 - t, NZ) if d == 0 else lax.rem(z + 1 + t, NZ)
                arrive(piece(c), ag_r.at[d, t])
                if t < last:
                    send(piece(c), piece(c), ag_s.at[d, t + 1], ag_r.at[d, t + 1], to[d])
                send(piece(c), piece(c), cc_s.at[1 + 2 * t + d], cc_r.at[c], sibling)
            yield

    def route(e):
        match = ids_ref[...] == e
        routed = jnp.sum(jnp.where(match, 1.0, 0.0), axis=1, keepdims=True)
        gate = jnp.sum(jnp.where(match, gates_ref[...], 0.0), axis=1, keepdims=True)
        rows = lax.broadcasted_iota(jnp.int32, (TOK, TOK), 0)
        lanes = lax.broadcasted_iota(jnp.int32, (TOK, TOK), 1)
        before = jnp.where(lanes < rows, 1.0, 0.0).astype(BF)
        wide = jnp.broadcast_to(routed, (TOK, TOK))
        rank = dot(before, wide.astype(BF))
        cap = jnp.where(e == 0, caps[0], caps[1]).astype(F32)
        kept = jnp.logical_and(wide > 0.5, rank < cap)
        slot = lanes.astype(F32)
        first = jnp.where(jnp.logical_and(kept, rank == slot), 1.0, 0.0)[:, : 2 * CAP]
        second = jnp.where(jnp.logical_and(kept, rank == slot - CAP), 1.0, 0.0)[:, : 2 * CAP]
        return first.astype(BF), second.astype(BF), gate

    def main():
        for i in range(NZ):
            arrive(wbuf.at[x, y, i, core], z_r.at[i])
        a_own = wbuf.at[x, y, pl.ds(0, 8), core]
        b_own = wbuf.at[x, y, pl.ds(8, 8), core]
        for i in range(1, 4):
            xx, yy = lax.rem(x + i, NX), lax.rem(y + i, NY)
            send(a_own, a_own, p1_s.at[0, i], p1_r.at[0, x], at(xx=xx))
            send(b_own, b_own, p1_s.at[1, i], p1_r.at[1, y], at(yy=yy))
        yield
        for i in range(1, 4):
            xx, yy = lax.rem(x + i, NX), lax.rem(y + i, NY)
            arrive(wbuf.at[xx, y, pl.ds(0, 8), core], p1_r.at[0, xx])
            arrive(wbuf.at[x, yy, pl.ds(8, 8), core], p1_r.at[1, yy])

        def a_slab(yy):
            return wbuf.at[:, yy, pl.ds(0, 8), core]

        def b_slab(xx):
            return wbuf.at[xx, :, pl.ds(8, 8), core]

        for i in range(1, 4):
            xx, yy = lax.rem(x + i, NX), lax.rem(y + i, NY)
            send(a_slab(y), a_slab(y), p2_s.at[0, i], p2_r.at[0, y], at(yy=yy))
            send(b_slab(x), b_slab(x), p2_s.at[1, i], p2_r.at[1, x], at(xx=xx))
        send(a_slab(y), a_slab(y), c_s.at[0, 0], c_r.at[0, y], sibling)
        send(b_slab(x), b_slab(x), c_s.at[1, 0], c_r.at[1, x], sibling)
        yield
        for b in range(4):
            for i in (2 * b, 2 * b + 1):
                for j in range(3):
                    arrive(qkv.at[j, i], q_r.at[j, i])
            n = (b + 1) * 256
            q = qkv[0, 2 * b:2 * b + 2].reshape(256, HD)
            k = qkv[1, : 2 * b + 2].reshape(n, HD)
            v = qkv[2, : 2 * b + 2].reshape(n, HD)
            s = dot(q, k, NT) * HD ** (-0.5)
            qpos = lax.broadcasted_iota(jnp.int32, (256, n), 0) + b * 256
            kpos = lax.broadcasted_iota(jnp.int32, (256, n), 1)
            s = jnp.where(kpos <= qpos, s, -jnp.inf)
            w = jnp.exp(s - jnp.max(s, axis=1, keepdims=True))
            total = jnp.sum(w, axis=1, keepdims=True)
            o = dot(w.astype(BF), v) / total
            abuf[2 * b:2 * b + 2] = o.astype(BF).reshape(2, 128, HD)
            yield
        mine = attd.at[:, cols(ctx * HD, HD)]
        for i in range(1, NCTX):
            peer = lax.rem(ctx + i, NCTX)
            send(abuf.at[peer], mine, a_s.at[i], a_r.at[ctx], (dp, peer))
        pltpu.make_async_copy(abuf.at[ctx], mine, a_r.at[ctx]).start()
        yield
        for i in range(1, 4):
            xx, yy = lax.rem(x + i, NX), lax.rem(y + i, NY)
            arrive(a_slab(yy), p2_r.at[0, yy])
            send(a_slab(yy), a_slab(yy), c_s.at[0, i], c_r.at[0, yy], sibling)
            arrive(b_slab(xx), p2_r.at[1, xx])
            send(b_slab(xx), b_slab(xx), c_s.at[1, i], c_r.at[1, xx], sibling)
            yield
        for i in range(NCTX):
            arrive(attd.at[:, i * HD:(i + 1) * HD], a_r.at[i])
        for i in range(4):
            arrive(wbuf.at[:, i, pl.ds(0, 8), 1 - core], c_r.at[0, i])
            arrive(wbuf.at[i, :, pl.ds(8, 8), 1 - core], c_r.at[1, i])
        res_copy.wait()
        squares = jnp.zeros((TOK, 1), F32)
        for i in range(NCTX):
            acc = dot(attd[:, :512], wbuf[(i // NY) * 2, i % NY].reshape(512, 256))
            acc += dot(attd[:, 512:], wbuf[(i // NY) * 2 + 1, i % NY].reshape(512, 256))
            out = acc.astype(BF)
            here = slice(i * 256, (i + 1) * 256)
            proj_ref[:, here] = out
            combined = res[:, here].astype(F32) + out.astype(F32)
            squares += jnp.sum(combined * combined, axis=1, keepdims=True)
            if i % 4 == 3:
                yield
        scale = lax.rsqrt(squares * (1.0 / D) + EPSILON)
        for i in range(NCTX):
            here = slice(i * 256, (i + 1) * 256)
            combined = res[:, here].astype(F32) + proj_ref[:, here].astype(F32)
            normed[:, here] = (combined * scale * gain_ref[:, here]).astype(BF)
        first, second, _ = route(1 - xl)
        dsend[...] = (dot(first, normed[:, :1024], TN) + dot(second, normed[:, 1024:], TN)).astype(BF)
        send(dsend, rbuf.at[ctx, xl], d_s, d_r, partner)
        first, second, _ = route(xl)
        rbuf[ctx, xl] = (dot(first, normed[:, :1024], TN) + dot(second, normed[:, 1024:], TN)).astype(BF)
        for i in range(1, NCTX):
            peer = lax.rem(ctx + i, NCTX)
            send(rbuf.at[ctx, xl], rbuf.at[ctx, xl], r_s.at[0, i], r_r.at[0, ctx], (dp, peer))
        yield
        arrive(rbuf.at[ctx, 1 - xl], d_r)
        for i in range(1, NCTX):
            peer = lax.rem(ctx + i, NCTX)
            send(rbuf.at[ctx, 1 - xl], rbuf.at[ctx, 1 - xl], r_s.at[1, i], r_r.at[1, ctx], (dp, peer))
        yield

    threads = {"w": weights(), "m": main()}
    alive = dict(threads)
    for step in SCHEDULE:
        if step in alive and next(alive[step], 0) == 0:
            del alive[step]
    for step in ("m", "w"):
        if step in alive:
            for _ in alive[step]:
                pass

    for c in range(NZ):
        arrive(wf.at[1 - core, :, c * 128:(c + 1) * 128], cc_r.at[c])
    uw[0:80] = wf[0, 176:256]
    uw[80:176] = wf[1, 0:96]
    for i in range(1, NCTX):
        peer = lax.rem(ctx + i, NCTX)
        arrive(rbuf.at[peer, xl], r_r.at[0, peer])
        arrive(rbuf.at[peer, 1 - xl], r_r.at[1, peer])
    for g in range(2):
        r = rbuf[4 * g:4 * g + 4].reshape(384, 1024)
        pair = []
        for w in (wf.at[0, 0:176], uw):
            left = dot(r, w[:, :1024], NT).reshape(8, 48, FF_DEV)
            right = dot(r, w[:, 1024:], NT).reshape(8, 48, FF_DEV)
            pair.append((left[:, :CAP] + right[:, CAP:]).reshape(8 * CAP, FF_DEV))
        gate_proj, up_proj = pair
        hidden = (gate_proj / (1.0 + jnp.exp(-gate_proj)) * up_proj).astype(BF)
        for h in range(2):
            out = dot(hidden, wf[1, 96:272, h * 1024:(h + 1) * 1024]).reshape(8, CAP, 1024)
            if h == 0:
                kept_left = out
        packed = jnp.concatenate([kept_left, out], axis=1).astype(BF)
        sbuf[4 * g:4 * g + 4] = packed.reshape(4, 2, 48, 1024)
    for i in range(1, NCTX):
        peer = lax.rem(ctx + i, NCTX)
        send(sbuf.at[peer], pbuf.at[ctx], e_s.at[i], e_r.at[ctx], (dp, peer))
    for i in range(1, NCTX):
        peer = lax.rem(ctx + i, NCTX)
        arrive(pbuf.at[peer], e_r.at[peer])

    def total_of(side):
        acc = sbuf[ctx, side].astype(F32)
        for i in range(1, NCTX):
            acc += pbuf[lax.rem(ctx + i, NCTX), side].astype(F32)
        return acc.astype(BF)

    xo[...] = total_of(1 - xl)
    send(xo, xi, o_s, o_r, partner)
    mine = total_of(xl)
    first, second, gate = route(xl)
    left = gate * dot(first, mine)
    right = gate * dot(second, mine)
    arrive(xi, o_r)
    theirs = xi[...]
    first, second, gate = route(1 - xl)
    sum_ref[:, :1024] = (left + gate * dot(first, theirs)).astype(BF)
    sum_ref[:, 1024:] = (right + gate * dot(second, theirs)).astype(BF)
    for copy in pending:
        copy.wait_send()


SCHEDULE = "wmwwmwwmwmwmwmwmwwmwmwmwmwwmwwmwwmwwmwwwwwww"


def body(
    query_vecs, key_vecs, value_vecs, residual, w_out, norm_gain, w_gate_up,
    w_down, expert_ids, route_gates, capacity, expert_owner,
):
    packed = jnp.concatenate(
        [w_gate_up[0, 0].T, w_gate_up[0, 1].T, w_down[0]], axis=0
    )
    hbm = pl.BlockSpec(memory_space=pl.ANY)
    vmem = pl.BlockSpec(memory_space=pltpu.VMEM)
    smem = pl.BlockSpec(memory_space=pltpu.SMEM)
    dma = pltpu.SemaphoreType.DMA
    out = jax.ShapeDtypeStruct((TOK, D), BF)
    rows = (2, 48, 1024)
    attn_proj, expert_sum = pl.pallas_call(
        kernel,
        out_shape=(out, out),
        in_specs=[smem, smem] + [hbm] * 6 + [vmem] * 3,
        out_specs=(vmem, vmem),
        scratch_shapes=[
            pltpu.VMEM((3, NCTX, TOK, HD), BF),
            pltpu.VMEM((NCTX, TOK, HD), BF),
            pltpu.VMEM((TOK, NCTX * HD), BF),
            pltpu.VMEM((NX, NY, NZ, 2, 16, 256), BF),
            pltpu.VMEM((TOK, D), BF),
            pltpu.VMEM((HALF, D), BF),
            pltpu.VMEM((HALF, D), BF),
            pltpu.VMEM((2, NZ, HALF, 128), BF),
            pltpu.VMEM((2, NZ - 1, HALF, 128), BF),
            pltpu.VMEM((HALF, 128), BF),
            pltpu.VMEM((2, HALF, D), BF),
            pltpu.VMEM((FF_DEV, D), BF),
            pltpu.VMEM((TOK, D), BF),
            pltpu.VMEM((NCTX,) + rows, BF),
            pltpu.VMEM(rows[1:], BF),
            pltpu.VMEM((NCTX,) + rows, BF),
            pltpu.VMEM((NCTX,) + rows, BF),
            pltpu.VMEM(rows[1:], BF),
            pltpu.VMEM(rows[1:], BF),
            dma((3, NCTX)), dma((3, NCTX)),
            dma((NCTX,)), dma((NCTX,)),
            dma((NZ,)), dma((NZ,)),
            dma((2, 4)), dma((2, 4)),
            dma((2, 4)), dma((2, 4)),
            dma((2, 4)), dma((2, 4)),
            dma((2,)), dma, dma,
            dma((2, NZ - 1)), dma((2, NZ - 1)),
            dma, dma,
            dma((2, 8)), dma((2, 8)),
            dma((NZ + 1,)), dma((NZ,)),
            dma, dma,
            dma((2, NCTX)), dma((2, NCTX)),
            dma((NCTX,)), dma((NCTX,)),
            dma, dma,
        ],
        compiler_params=pltpu.CompilerParams(
            collective_id=0, has_side_effects=True, vmem_limit_bytes=58 << 20
        ),
    )(
        expert_owner[:2], capacity[0, 0],
        query_vecs[0], key_vecs[0], value_vecs[0], residual[0], w_out, packed,
        norm_gain[None], expert_ids[0], route_gates[0],
    )
    return (attn_proj[None], expert_sum[None])


def solution(mesh):
    seq = P("dp", "ctx", None)
    placed = (
        seq, seq, seq, seq, P("dp", None), P(),
        P("dp", None, None, "ctx"), seq, seq, seq, seq, P(),
    )
    return jax.shard_map(
        body, mesh=mesh, in_specs=placed, out_specs=(seq, seq), check_vma=False
    )
```

time: 891 us -> 158 us (0.18)
  waiting for transfers between devices: 835 us -> 0 us
  Pallas kernels: 0 us -> 148 us
  matrix products: 16 us -> 0 us
  between operations: 15.7 us -> 0.65 us
  other arithmetic: 11.1 us -> 1.51 us
    psum x1 -> x0, waiting for transfers between devices: 433 us -> none  [broadcast(): return lax.psum(jnp.where(mine, array, jnp.zeros_like(array)), axis)]
    all_gather x4 -> x0, waiting for transfers between devices: 312 us -> none  [the longest x1 122 us: body(): lax.all_gather(w_out, 'dp', axis=0, tiled=True)]
    pallas_call x0 -> x1, Pallas kernels: none -> 148 us  [body(): pl.pallas_call(kernel, out_shape=(out, out), in_specs=[smem, smem] + [hbm...]
    unnamed x7 -> x0, waiting for transfers between devices: 89.7 us -> none
    dot_general x9 -> x0, matrix products: 16 us -> none  [the longest x2 4.71 us: body(): jnp.dot(hidden, down_part, preferred_element_type=jnp.float32)]
  transfers between devices with their start and end apart: 6 -> 0, of which waited for: 6 -> 0; matrix products, arithmetic and copies ran while one was open for 3% -> 0% of each run, Pallas kernels for 0% -> 0%
where the time goes in v1:
time: 158 us; the launch traced here: 157 us
  Pallas kernels  148 us (94%)
  local copies, waits for them, and re-layouts  6.78 us (4%)
    pallas_call x1, Pallas kernels, body(): pl.pallas_call(kernel, out_shape=(out, out), in_specs=[smem, smem] + [hbm...  148 us
    unnamed x10, local copies, waits for them, and re-layouts  5.29 us

profile of v1, /device:TPU:25, one launch (start us, length us, event | category | flops | bytes accessed | tf_op | source)
XLA Modules:
  0.0 157.4 jit_solution(13474110556114179701)
XLA Ops:
  0.6 0.0 copy-start
  0.6 1.5 slice_bitcast_fusion.1
  2.1 0.0 copy-done
  2.2 0.0 copy-start.1
  2.2 0.0 copy-start.2
  2.2 1.5 pad_maximum_fusion.w_ref
  3.7 0.0 copy-done.1
  3.7 0.7 copy.14
  4.4 0.0 copy-done.2
  4.4 0.7 copy.15
  5.2 148.4 %shard_map.131 = (bf16[128,2048]{1,0:T(8,128)(2,1)}, bf16[128,2048]{1,0:T(8,128)(2,1)}) custom-call(s32[2]{0:T(128)} %bitcast.30, s32[2]{0:T(128)} %bitcast.31, bf16[128,1024]{1,0:T(8,128)(2,1)} %bitcast.26, bf16[128,1024]{1,0:T(8,128)(2,1)} %bitcast.27, bf16[128,1024]{1,0:T(8,128)(2,1)} %bitcast.28, bf16[128,2048]{1,0:T(8,128)(2,1)} %bitcast.23, ...), custom_call_target="tpu_custom_call" | custom-call | tf_op jit(solution)/shard_map/pallas_call | solution.py:351
  153.6 1.9 %copy.18 = bf16[1,128,2048]{2,1,0:T(8,128)(2,1)} copy(bf16[1,128,2048]{2,1,0:T(8,128)(2,1)} %bitcast.22) | data formatting | bytes 1048576
  155.5 1.9 %copy.19 = bf16[1,128,2048]{2,1,0:T(8,128)(2,1)} copy(bf16[1,128,2048]{2,1,0:T(8,128)(2,1)} %bitcast.21) | data formatting | bytes 1048576
Async XLA Ops:
  0.6 1.5 copy-start
  2.2 1.5 copy-start.1
  2.2 2.3 %copy-start.2 = (f32[1,128,6]{1,0,2:T(1,128)S(1)}, f32[1,128,6]{1,0,2:T(1,128)}, u32[]{:S(2)}) copy-start(f32[1,128,6]{1,0,2:T(1,128)} %param.21) | copy-start | bytes 9220

commit v2 on v1

v2 whole, which is shorter than its diff:
```python
import jax
import jax.numpy as jnp
from jax import lax
from jax.experimental import pallas as pl
from jax.experimental.pallas import tpu as pltpu
from jax.sharding import PartitionSpec as P

D = 2048
HD = 128
FF_DEV = 176
CAP = 24
TOK = 128
PICKS = 6
NZ = 16
NY = 4
NX = 4
NCTX = 8
HALF = 272
HALF_STEP = 256
HOPS = NZ // 2
EPSILON = 1e-06
MESH = pl.DeviceIdType.MESH
BF = jnp.bfloat16
F32 = jnp.float32

NN = (((1,), (0,)), ((), ()))
NT = (((1,), (1,)), ((), ()))
TN = (((0,), (0,)), ((), ()))

SCHEDULE = "wmwmwmmwmmmwwmwmmwmmwmwwwwwwwwww"
GROUPS = ((1, 2, 3, 4), (5, 6, 7, 0))
AG_PARTS = ((0, 144), (144, 128))


def dot(a, b, dims=NN):
    return lax.dot_general(a, b, dims, preferred_element_type=F32)


def cols(start, size):
    return pl.ds(pl.multiple_of(start, 128), size)


def slot_rows(ids_ref, cap, e):
    routed = jnp.zeros((1, TOK), F32)
    for i in range(PICKS):
        routed += jnp.where(ids_ref[i] == e, 1.0, 0.0)
    rows = lax.broadcasted_iota(jnp.int32, (TOK, TOK), 0)
    lanes = lax.broadcasted_iota(jnp.int32, (TOK, TOK), 1)
    before = jnp.where(rows < lanes, 1.0, 0.0).astype(BF)
    rank = dot(jnp.broadcast_to(routed, (8, TOK)).astype(BF), before)[0:1]
    kept = jnp.where(rank < cap.astype(F32), routed, 0.0)
    rank = jnp.where(kept > 0.5, rank, -1000.0)
    slot = lax.broadcasted_iota(jnp.int32, (2 * CAP, TOK), 0).astype(F32)
    first = jnp.where(rank == slot, 1.0, 0.0)
    second = jnp.where(rank == slot - CAP, 1.0, 0.0)
    return first, second


def kernel(
    owner, caps,
    q_ref, k_ref, v_ref, res_ref, wo_ref, wg_ref, wd_ref, gain_ref, ids_ref,
    proj_ref, tot_ref,
    qkv, abuf, attd, wbuf, res, packed, oth, cand, rsb, xsend, xpiece, wf, uw,
    normed, rbuf, dsend, sbuf, pbuf,
    q_s, q_r, a_s, a_r, z_s, z_r, p1_s, p1_r, p2_s, p2_r, c_s, c_r,
    l_s, oth_s, oth_r, rs_s, rs_r, xp_s, xp_r, ag_s, ag_r, cc_s, cc_r,
    r_s, r_r, e_s, e_r,
):
    dp = lax.axis_index("dp")
    ctx = lax.axis_index("ctx")
    core = lax.rem(dp, 2)
    z = lax.rem(dp // 2, NZ)
    xl = dp // (2 * NZ)
    xh = ctx // NY
    y = lax.rem(ctx, NY)
    x = xh * 2 + xl

    def at(xx=None, yy=None, zz=None, cc=None):
        xx = x if xx is None else xx
        yy = y if yy is None else yy
        zz = z if zz is None else zz
        cc = core if cc is None else cc
        return ((lax.rem(xx, 2) * NZ + zz) * 2 + cc, (xx // 2) * NY + yy)

    line = dp + 2 * NZ * (1 - 2 * xl)
    partner = (line, ctx)
    sibling = at(cc=1 - core)
    up = at(zz=lax.rem(z + 1, NZ))
    down = at(zz=lax.rem(z + NZ - 1, NZ))

    def peer(i):
        return lax.rem(ctx + i, NCTX)

    def send(src, dst, ssem, rsem, dev):
        pltpu.make_async_remote_copy(
            src_ref=src, dst_ref=dst, send_sem=ssem, recv_sem=rsem,
            device_id=dev, device_id_type=MESH,
        ).start()

    def local(src, dst, sem):
        pltpu.make_async_copy(src, dst, sem).start()

    def arrive(dst, sem):
        pltpu.make_async_copy(dst, dst, sem).wait()

    barrier = pltpu.get_barrier_semaphore()
    partners = [sibling]
    partners += [at(zz=lax.rem(z + i, NZ)) for i in range(1, NZ)]
    partners += [(dp, peer(i)) for i in range(1, NCTX)]
    partners += [(line, peer(i)) for i in range(NCTX)]
    for dev in partners:
        pl.semaphore_signal(barrier, inc=1, device_id=dev, device_id_type=MESH)
    local(wg_ref.at[0], packed.at[0:176], l_s.at[0])
    local(wg_ref.at[1], packed.at[176:352], l_s.at[0])
    local(wd_ref, packed.at[352:528], l_s.at[0])
    local(res_ref, res, l_s.at[1])
    arrive(packed, l_s.at[0])
    pl.semaphore_wait(barrier, len(partners))

    other_rows = pl.ds(pl.multiple_of((1 - core) * HALF_STEP, 16), HALF)
    send(packed.at[other_rows, :], oth, oth_s, oth_r, sibling)
    wo_part = wo_ref.at[:, cols(ctx * 256, 256)]
    for i in range(1, NZ):
        send(wo_part, wbuf.at[x, y, z, core], z_s, z_r, at(zz=lax.rem(z + i, NZ)))
    local(wo_part, wbuf.at[x, y, z, core], z_r)
    for i in range(1, NCTX):
        for j, ref in enumerate((q_ref, k_ref, v_ref)):
            send(ref.at[:, cols(peer(i) * HD, HD)], qkv.at[j, ctx], q_s, q_r.at[ctx], (dp, peer(i)))
    for j, ref in enumerate((q_ref, k_ref, v_ref)):
        local(ref.at[:, cols(ctx * HD, HD)], qkv.at[j, ctx], q_r.at[ctx])

    owners = (owner[0], owner[1])

    def weights():
        arrive(oth, oth_r)
        mate = dp + 1 - 2 * core
        own_rows = pl.ds(pl.multiple_of(core * HALF_STEP, 16), HALF)
        has = []
        for e in range(2):
            mine = owners[e] == dp
            mates = owners[e] == mate
            has.append(jnp.logical_or(mine, mates))
            for c in range(NZ):
                a = packed[own_rows, c * 128:(c + 1) * 128]
                b = oth[:, c * 128:(c + 1) * 128]
                cand[e, c] = lax.select(mine, a, lax.select(mates, b, jnp.zeros_like(b)))
        to = (up, down)
        for d in range(2):
            c = lax.rem(z + 8, NZ) if d == 0 else lax.rem(z + 9, NZ)
            for e in range(2):
                send(cand.at[e, c], rsb.at[e, HOPS * d], rs_s, rs_r.at[e, HOPS * d], to[d])
        yield
        for t in range(HOPS):
            for d in range(2):
                last = HOPS - 1 - d
                if t > last:
                    continue
                slot = HOPS * d + t
                c = lax.rem(z + 7 - t, NZ) if d == 0 else lax.rem(z + 10 + t, NZ)
                for e in range(2):
                    arrive(rsb.at[e, slot], rs_r.at[e, slot])
                    if t < last:
                        rsb[e, slot] = lax.select(has[e], cand[e, c], rsb[e, slot])
                        send(rsb.at[e, slot], rsb.at[e, slot + 1], rs_s, rs_r.at[e, slot + 1], to[d])
            yield

        def settled(e, known):
            met = rsb[e, HOPS - 1] + rsb[e, 2 * HOPS - 2]
            return lax.select(known, cand[e, z], met)

        known = jnp.where(xl == 0, has[1].astype(jnp.int32), has[0].astype(jnp.int32)) > 0
        xsend[...] = settled(1 - xl, known)
        send(xsend, xpiece, xp_s, xp_r, partner)
        known = jnp.where(xl == 0, has[0].astype(jnp.int32), has[1].astype(jnp.int32)) > 0
        here = settled(xl, known)
        arrive(xpiece, xp_r)
        wf[core, :, cols(z * 128, 128)] = here + xpiece[...]

        def piece(c):
            return wf.at[core, :, cols(c * 128, 128)]

        def part(c, h):
            return wf.at[core, pl.ds(AG_PARTS[h][0], AG_PARTS[h][1]), cols(c * 128, 128)]

        for h in range(2):
            for d in range(2):
                send(part(z, h), part(z, h), ag_s, ag_r.at[d, 0, h], to[d])
        send(piece(z), piece(z), cc_s, cc_r, sibling)
        yield
        for t in range(HOPS):
            for d in range(2):
                last = HOPS - 1 - d
                if t > last:
                    continue
                c = lax.rem(z + NZ - 1 - t, NZ) if d == 0 else lax.rem(z + 1 + t, NZ)
                for h in range(2):
                    arrive(part(c, h), ag_r.at[d, t, h])
                    if t < last:
                        send(part(c, h), part(c, h), ag_s, ag_r.at[d, t + 1, h], to[d])
                send(piece(c), piece(c), cc_s, cc_r, sibling)
            yield

    def a_slab(yy):
        return wbuf.at[:, yy, pl.ds(0, 8), core]

    def b_slab(xx):
        return wbuf.at[xx, :, pl.ds(8, 8), core]

    def main():
        arrive(wbuf.at[x, y, :, core], z_r)
        a_own = wbuf.at[x, y, pl.ds(0, 8), core]
        b_own = wbuf.at[x, y, pl.ds(8, 8), core]
        for i in range(1, 4):
            send(a_own, a_own, p1_s, p1_r.at[0], at(xx=lax.rem(x + i, NX)))
            send(b_own, b_own, p1_s, p1_r.at[1], at(yy=lax.rem(y + i, NY)))
        yield
        three = wbuf.at[pl.ds(0, 3), 0, pl.ds(0, 8), 0]
        arrive(three, p1_r.at[0])
        arrive(three, p1_r.at[1])
        for i in range(1, 4):
            send(a_slab(y), a_slab(y), p2_s, p2_r.at[0, y], at(yy=lax.rem(y + i, NY)))
            send(b_slab(x), b_slab(x), p2_s, p2_r.at[1, x], at(xx=lax.rem(x + i, NX)))
        send(a_slab(y), a_slab(y), c_s, c_r, sibling)
        send(b_slab(x), b_slab(x), c_s, c_r, sibling)
        yield
        for b in range(4):
            for i in (2 * b, 2 * b + 1):
                arrive(qkv.at[:, i], q_r.at[i])
            n = (b + 1) * 256
            q = qkv[0, 2 * b:2 * b + 2].reshape(256, HD)
            k = qkv[1, : 2 * b + 2].reshape(n, HD)
            v = qkv[2, : 2 * b + 2].reshape(n, HD)
            s = dot(q, k, NT) * HD ** (-0.5)
            qpos = lax.broadcasted_iota(jnp.int32, (256, n), 0) + b * 256
            kpos = lax.broadcasted_iota(jnp.int32, (256, n), 1)
            s = jnp.where(kpos <= qpos, s, -jnp.inf)
            w = jnp.exp(s - jnp.max(s, axis=1, keepdims=True))
            total = jnp.sum(w, axis=1, keepdims=True)
            o = dot(w.astype(BF), v) / total
            abuf[2 * b:2 * b + 2] = o.astype(BF).reshape(2, 128, HD)
            yield
        mine = attd.at[:, cols(ctx * HD, HD)]
        for i in range(1, NCTX):
            send(abuf.at[peer(i)], mine, a_s, a_r, (dp, peer(i)))
        local(abuf.at[ctx], mine, a_r)
        yield
        for i in (1, 3, 2):
            xx, yy = lax.rem(x + i, NX), lax.rem(y + i, NY)
            arrive(a_slab(yy), p2_r.at[0, yy])
            send(a_slab(yy), a_slab(yy), c_s, c_r, sibling)
            arrive(b_slab(xx), p2_r.at[1, xx])
            send(b_slab(xx), b_slab(xx), c_s, c_r, sibling)
            yield
        arrive(attd, a_r)
        arrive(res, l_s.at[1])
        arrive(wbuf.at[:, :, :, 1 - core], c_r)
        squares = jnp.zeros((TOK, 1), F32)
        for i in range(NCTX):
            acc = dot(attd[:, :512], wbuf[(i // NY) * 2, i % NY].reshape(512, 256))
            acc += dot(attd[:, 512:], wbuf[(i // NY) * 2 + 1, i % NY].reshape(512, 256))
            out = acc.astype(BF)
            here = slice(i * 256, (i + 1) * 256)
            proj_ref[:, here] = out
            combined = res[:, here].astype(F32) + out.astype(F32)
            squares += jnp.sum(combined * combined, axis=1, keepdims=True)
            if i % 4 == 3:
                yield
        scale = lax.rsqrt(squares * (1.0 / D) + EPSILON)
        for i in range(NCTX):
            here = slice(i * 256, (i + 1) * 256)
            combined = res[:, here].astype(F32) + proj_ref[:, here].astype(F32)
            normed[:, here] = (combined * scale * gain_ref[:, here]).astype(BF)
        for e, dst in ((xl, rbuf.at[xl, ctx]), (1 - xl, dsend)):
            first, second = slot_rows(ids_ref, jnp.where(e == 0, caps[0], caps[1]), e)
            rows = dot(first.astype(BF), normed[:, :1024]) + dot(second.astype(BF), normed[:, 1024:])
            dst[...] = rows.astype(BF)
        slot = rbuf.at[xl, ctx]
        for i in (4, 5, 6, 7, 1, 2, 3, 0):
            group = 0 if i >= 4 else 1
            if i:
                send(slot, slot, r_s.at[0], r_r.at[group], (dp, peer(i)))
            send(dsend, slot, r_s.at[1], r_r.at[group], (line, peer(i)))
        yield

    threads = {"w": weights(), "m": main()}
    for step in SCHEDULE:
        next(threads[step], 0)
    for step in ("m", "w"):
        for _ in threads[step]:
            pass

    arrive(wf.at[1 - core], cc_r)
    uw[0:80] = wf[0, 176:256]
    uw[80:176] = wf[1, 0:96]
    for g, group in enumerate(GROUPS):
        arrive(rbuf.at[0, pl.ds(0, 8 - g)], r_r.at[g])
        r = jnp.concatenate(
            [rbuf[s, peer(i)] for i in group for s in (xl, 1 - xl)], axis=0
        )
        pair = []
        for w in (wf.at[0, 0:176], uw):
            left = dot(r, w[:, :1024], NT).reshape(8, 48, FF_DEV)
            right = dot(r, w[:, 1024:], NT).reshape(8, 48, FF_DEV)
            pair.append((left[:, :CAP] + right[:, CAP:]).reshape(8 * CAP, FF_DEV))
        gate_proj, up_proj = pair
        hidden = (gate_proj / (1.0 + jnp.exp(-gate_proj)) * up_proj).astype(BF)
        halves = [
            dot(hidden, wf[1, 96:272, h * 1024:(h + 1) * 1024]).reshape(8, CAP, 1024)
            for h in range(2)
        ]
        out = jnp.concatenate(halves, axis=1).astype(BF)
        for j, i in enumerate(group):
            for s in range(2):
                sbuf[s, i] = out[2 * j + s]
        for i in group:
            if i:
                send(sbuf.at[0, i], pbuf.at[xl, ctx], e_s.at[0], e_r.at[0], (dp, peer(i)))
            send(sbuf.at[1, i], pbuf.at[xl, ctx], e_s.at[1], e_r.at[1], (line, peer(i)))

    arrive(pbuf.at[0, pl.ds(0, 7)], e_r.at[0])
    acc = sbuf[0, 0].astype(F32)
    for i in range(1, NCTX):
        acc += pbuf[xl, peer(i)].astype(F32)
    tot_ref[xl] = acc.astype(BF)
    arrive(pbuf.at[0], e_r.at[1])
    acc = pbuf[1 - xl, 0].astype(F32)
    for i in range(1, NCTX):
        acc += pbuf[1 - xl, i].astype(F32)
    tot_ref[1 - xl] = acc.astype(BF)

    arrive(oth, oth_s)
    arrive(wbuf.at[0, 0, pl.ds(0, NZ - 1), 0], z_s)
    arrive(qkv.at[:, pl.ds(0, NCTX - 1)], q_s)
    arrive(abuf.at[pl.ds(0, NCTX - 1)], a_s)
    arrive(wbuf.at[pl.ds(0, 3), pl.ds(0, 2), pl.ds(0, 8), 0], p1_s)
    arrive(wbuf.at[pl.ds(0, 3), :, :, 0], p2_s)
    arrive(wbuf.at[:, :, :, 0], c_s)
    arrive(rsb, rs_s)
    arrive(xsend, xp_s)
    arrive(wf.at[0, :, pl.ds(0, 15 * 128)], ag_s)
    arrive(wf.at[0], cc_s)
    for sems, buf in ((r_s, rbuf), (e_s, pbuf)):
        arrive(buf.at[0, pl.ds(0, 7)], sems.at[0])
        arrive(buf.at[0], sems.at[1])


def combine(caps, ids_ref, gates_ref, tot_ref, proj_ref, out_ref, sum_ref, sem):
    copy = pltpu.make_async_copy(proj_ref, out_ref, sem)
    copy.start()
    firsts, seconds, rows = [], [], []
    for e in range(2):
        gate = jnp.zeros((1, TOK), F32)
        for i in range(PICKS):
            gate += jnp.where(ids_ref[i] == e, gates_ref[i], 0.0)
        high = gate.astype(BF).astype(F32)
        first, second = slot_rows(ids_ref, caps[e], e)
        for g in (high, gate - high):
            firsts.append(first * g)
            seconds.append(second * g)
            rows.append(tot_ref[e])
    rows = jnp.concatenate(rows, axis=0)
    sum_ref[:, :1024] = dot(jnp.concatenate(firsts, axis=0).astype(BF), rows, TN).astype(BF)
    sum_ref[:, 1024:] = dot(jnp.concatenate(seconds, axis=0).astype(BF), rows, TN).astype(BF)
    copy.wait()


def body(
    query_vecs, key_vecs, value_vecs, residual, w_out, norm_gain, w_gate_up,
    w_down, expert_ids, route_gates, capacity, expert_owner,
):
    hbm = pl.BlockSpec(memory_space=pl.ANY)
    vmem = pl.BlockSpec(memory_space=pltpu.VMEM)
    smem = pl.BlockSpec(memory_space=pltpu.SMEM)
    dma = pltpu.SemaphoreType.DMA
    out = jax.ShapeDtypeStruct((TOK, D), BF)
    rows = (2 * CAP, 1024)
    ids = jnp.transpose(expert_ids, (2, 0, 1))
    gates = jnp.transpose(route_gates, (2, 0, 1))
    proj, tot = pl.pallas_call(
        kernel,
        out_shape=(out, jax.ShapeDtypeStruct((2,) + rows, BF)),
        in_specs=[smem, smem] + [hbm] * 7 + [vmem] * 2,
        out_specs=(vmem, vmem),
        scratch_shapes=[
            pltpu.VMEM((3, NCTX, TOK, HD), BF),
            pltpu.VMEM((NCTX, TOK, HD), BF),
            pltpu.VMEM((TOK, NCTX * HD), BF),
            pltpu.VMEM((NX, NY, NZ, 2, 16, 256), BF),
            pltpu.VMEM((TOK, D), BF),
            pltpu.VMEM((3 * FF_DEV, D), BF),
            pltpu.VMEM((HALF, D), BF),
            pltpu.VMEM((2, NZ, HALF, 128), BF),
            pltpu.VMEM((2, NZ - 1, HALF, 128), BF),
            pltpu.VMEM((HALF, 128), BF),
            pltpu.VMEM((HALF, 128), BF),
            pltpu.VMEM((2, HALF, D), BF),
            pltpu.VMEM((FF_DEV, D), BF),
            pltpu.VMEM((TOK, D), BF),
            pltpu.VMEM((2, NCTX) + rows, BF),
            pltpu.VMEM(rows, BF),
            pltpu.VMEM((2, NCTX) + rows, BF),
            pltpu.VMEM((2, NCTX) + rows, BF),
            dma, dma((NCTX,)), dma, dma, dma, dma,
            dma, dma((2,)), dma, dma((2, 4)), dma, dma,
            dma((2,)), dma, dma, dma, dma((2, NZ - 1)), dma, dma,
            dma, dma((2, HOPS, 2)), dma, dma,
            dma((2,)), dma((2,)), dma((2,)), dma((2,)),
        ],
        compiler_params=pltpu.CompilerParams(
            collective_id=0, has_side_effects=True, vmem_limit_bytes=58 << 20
        ),
    )(
        expert_owner[:2], capacity[0, 0],
        query_vecs[0], key_vecs[0], value_vecs[0], residual[0], w_out,
        jnp.swapaxes(w_gate_up[0], 1, 2), w_down[0], norm_gain[None], ids,
    )
    attn_proj, expert_sum = pl.pallas_call(
        combine,
        out_shape=(out, out),
        in_specs=[smem, vmem, vmem, vmem, hbm],
        out_specs=(hbm, vmem),
        scratch_shapes=[dma],
    )(capacity[0, 0], ids, gates, tot, proj)
    return (attn_proj[None], expert_sum[None])


def solution(mesh):
    seq = P("dp", "ctx", None)
    placed = (
        seq, seq, seq, seq, P("dp", None), P(),
        P("dp", None, None, "ctx"), seq, seq, seq, seq, P(),
    )
    return jax.shard_map(
        body, mesh=mesh, in_specs=placed, out_specs=(seq, seq), check_vma=False
    )
```

time: 158 us -> 152 us (0.962)
  local copies, waits for them, and re-layouts: 6.78 us -> 0 us
    unnamed x10 -> x0, local copies, waits for them, and re-layouts: 5.29 us -> none
    pallas_call x1 -> x2, Pallas kernels: 148 us -> 149 us  [the longest x1 131 us: body(): pl.pallas_call(kernel, out_shape=(out, jax.ShapeDtypeStruct((2,) + rows,...]
where the time goes in v2:
time: 152 us; the launch traced here: 150 us
  Pallas kernels  149 us (98%)
    pallas_call x1, Pallas kernels, body(): pl.pallas_call(kernel, out_shape=(out, jax.ShapeDtypeStruct((2,) + rows,...  131 us
    pallas_call x1, Pallas kernels, body(): pl.pallas_call(combine, out_shape=(out, out), in_specs=[smem, vmem, vmem,...  18.8 us

profile of v2, /device:TPU:25, one launch (start us, length us, event | category | flops | bytes accessed | tf_op | source)
XLA Modules:
  0.0 149.9 jit_solution(16459775789270598224)
XLA Ops:
  0.6 130.5 %shard_map.131 = (bf16[128,2048]{1,0:T(8,128)(2,1)}, bf16[2,48,1024]{2,1,0:T(8,128)(2,1)}) custom-call(s32[2]{0:T(128)} %bitcast.27, s32[2]{0:T(128)} %bitcast.25, bf16[128,1024]{1,0:T(8,128)(2,1)} %bitcast.18, bf16[128,1024]{1,0:T(8,128)(2,1)} %bitcast.19, bf16[128,1024]{1,0:T(8,128)(2,1)} %bitcast.20, bf16[128,2048]{1,0:T(8,128)(2,1)} %bitcast.17, ...), custom_call_target="tpu_custom_call" | custom-call | tf_op jit(solution)/shard_map/pallas_call | solution.py:379
  131.2 18.8 %shard_map.132 = (bf16[128,2048]{1,0:T(8,128)(2,1)}, bf16[128,2048]{1,0:T(8,128)(2,1)}) custom-call(s32[2]{0:T(128)} %bitcast.26, s32[6,1,128]{2,1,0:T(1,128)} %bitcast.22, f32[6,1,128]{2,1,0:T(1,128)} %bitcast.24, bf16[2,48,1024]{2,1,0:T(8,128)(2,1)} %get-tuple-element.6.tot_ref, bf16[128,2048]{1,0:T(8,128)(2,1)} %get-tuple-element.7.proj_ref), custom_call_target="tpu_custom_call" | custom-call | tf_op jit(solution)/shard_map/pallas_call | solution.py:417

commit v3 on v2

--- a/solution.py
+++ b/solution.py
@@ -27,13 +27,17 @@
 NT = (((1,), (1,)), ((), ()))
 TN = (((0,), (0,)), ((), ()))
 
-SCHEDULE = "wmwmwmmwmmmwwmwmmwmmwmwwwwwwwwww"
+SCHEDULE = "wmwmwmwmmmmwmmmwmwmwmmmwwmwmwmwmwmwmwmwmw"
 GROUPS = ((1, 2, 3, 4), (5, 6, 7, 0))
-AG_PARTS = ((0, 144), (144, 128))
+PARTS = ((0, 144), (144, 128))
 
 
 def dot(a, b, dims=NN):
     return lax.dot_general(a, b, dims, preferred_element_type=F32)
+
+
+def span(h):
+    return pl.ds(*PARTS[h])
 
 
 def cols(start, size):
@@ -148,7 +152,9 @@
         for d in range(2):
             c = lax.rem(z + 8, NZ) if d == 0 else lax.rem(z + 9, NZ)
             for e in range(2):
-                send(cand.at[e, c], rsb.at[e, HOPS * d], rs_s, rs_r.at[e, HOPS * d], to[d])
+                for h in range(2):
+                    dst = rsb.at[e, HOPS * d, span(h)]
+                    send(cand.at[e, c, span(h)], dst, rs_s, rs_r.at[e, HOPS * d, h], to[d])
         yield
         for t in range(HOPS):
             for d in range(2):
@@ -158,10 +164,12 @@
                 slot = HOPS * d + t
                 c = lax.rem(z + 7 - t, NZ) if d == 0 else lax.rem(z + 10 + t, NZ)
                 for e in range(2):
-                    arrive(rsb.at[e, slot], rs_r.at[e, slot])
-                    if t < last:
-                        rsb[e, slot] = lax.select(has[e], cand[e, c], rsb[e, slot])
-                        send(rsb.at[e, slot], rsb.at[e, slot + 1], rs_s, rs_r.at[e, slot + 1], to[d])
+                    for h in range(2):
+                        got = rsb.at[e, slot, span(h)]
+                        arrive(got, rs_r.at[e, slot, h])
+                        if t < last:
+                            got[...] = lax.select(has[e], cand[e, c, span(h)], got[...])
+                            send(got, rsb.at[e, slot + 1, span(h)], rs_s, rs_r.at[e, slot + 1, h], to[d])
             yield
 
         def settled(e, known):
@@ -179,24 +187,34 @@
         def piece(c):
             return wf.at[core, :, cols(c * 128, 128)]
 
-        def part(c, h):
-            return wf.at[core, pl.ds(AG_PARTS[h][0], AG_PARTS[h][1]), cols(c * 128, 128)]
-
-        for h in range(2):
-            for d in range(2):
-                send(part(z, h), part(z, h), ag_s, ag_r.at[d, 0, h], to[d])
+        far = (at(zz=lax.rem(z + 2, NZ)), at(zz=lax.rem(z + NZ - 2, NZ)))
+
+        def onward(c, d, t):
+            if t < HOPS // 2 - d:
+                send(piece(c), piece(c), ag_s.at[0], ag_r.at[d, 2 * t + 1], far[d])
+            if t < HOPS // 2:
+                send(piece(c), piece(c), ag_s.at[1], ag_r.at[d, 2 * t], to[d])
+            send(piece(c), piece(c), cc_s, cc_r, sibling)
+
+        def source(d, hops):
+            return lax.rem(z + (NZ - hops if d == 0 else hops), NZ)
+
+        for d in range(2):
+            send(piece(z), piece(z), ag_s.at[0], ag_r.at[d, 1], far[d])
+        for d in range(2):
+            send(piece(z), piece(z), ag_s.at[1], ag_r.at[d, 0], to[d])
         send(piece(z), piece(z), cc_s, cc_r, sibling)
         yield
-        for t in range(HOPS):
+        for t in range(1, HOPS // 2 + 1):
             for d in range(2):
-                last = HOPS - 1 - d
-                if t > last:
-                    continue
-                c = lax.rem(z + NZ - 1 - t, NZ) if d == 0 else lax.rem(z + 1 + t, NZ)
-                for h in range(2):
-                    arrive(part(c, h), ag_r.at[d, t, h])
-                    if t < last:
-                        send(part(c, h), part(c, h), ag_s, ag_r.at[d, t + 1, h], to[d])
+                if t <= HOPS // 2 - d:
+                    c = source(d, 2 * t)
+                    arrive(piece(c), ag_r.at[d, 2 * t - 1])
+                    onward(c, d, t)
+            yield
+            for d in range(2):
+                c = source(d, 2 * t - 1)
+                arrive(piece(c), ag_r.at[d, 2 * t - 2])
                 send(piece(c), piece(c), cc_s, cc_r, sibling)
             yield
 
@@ -217,9 +235,10 @@
         three = wbuf.at[pl.ds(0, 3), 0, pl.ds(0, 8), 0]
         arrive(three, p1_r.at[0])
         arrive(three, p1_r.at[1])
-        for i in range(1, 4):
+        for i in (1, 3, 2):
             send(a_slab(y), a_slab(y), p2_s, p2_r.at[0, y], at(yy=lax.rem(y + i, NY)))
             send(b_slab(x), b_slab(x), p2_s, p2_r.at[1, x], at(xx=lax.rem(x + i, NX)))
+            yield
         send(a_slab(y), a_slab(y), c_s, c_r, sibling)
         send(b_slab(x), b_slab(x), c_s, c_r, sibling)
         yield
@@ -280,7 +299,7 @@
             if i:
                 send(slot, slot, r_s.at[0], r_r.at[group], (dp, peer(i)))
             send(dsend, slot, r_s.at[1], r_r.at[group], (line, peer(i)))
-        yield
+            yield
 
     threads = {"w": weights(), "m": main()}
     for step in SCHEDULE:
@@ -337,16 +356,16 @@
     arrive(wbuf.at[:, :, :, 0], c_s)
     arrive(rsb, rs_s)
     arrive(xsend, xp_s)
-    arrive(wf.at[0, :, pl.ds(0, 15 * 128)], ag_s)
+    arrive(wf.at[0, :, pl.ds(0, 7 * 128)], ag_s.at[0])
+    arrive(wf.at[0, :, pl.ds(0, 8 * 128)], ag_s.at[1])
     arrive(wf.at[0], cc_s)
     for sems, buf in ((r_s, rbuf), (e_s, pbuf)):
         arrive(buf.at[0, pl.ds(0, 7)], sems.at[0])
         arrive(buf.at[0], sems.at[1])
 
 
-def combine(caps, ids_ref, gates_ref, tot_ref, proj_ref, out_ref, sum_ref, sem):
-    copy = pltpu.make_async_copy(proj_ref, out_ref, sem)
-    copy.start()
+def combine(caps, ids_ref, gates_ref, tot_ref, proj_ref, out_ref, sum_ref):
+    out_ref[...] = proj_ref[...]
     firsts, seconds, rows = [], [], []
     for e in range(2):
         gate = jnp.zeros((1, TOK), F32)
@@ -361,7 +380,6 @@
     rows = jnp.concatenate(rows, axis=0)
     sum_ref[:, :1024] = dot(jnp.concatenate(firsts, axis=0).astype(BF), rows, TN).astype(BF)
     sum_ref[:, 1024:] = dot(jnp.concatenate(seconds, axis=0).astype(BF), rows, TN).astype(BF)
-    copy.wait()
 
 
 def body(
@@ -402,8 +420,8 @@
             pltpu.VMEM((2, NCTX) + rows, BF),
             dma, dma((NCTX,)), dma, dma, dma, dma,
             dma, dma((2,)), dma, dma((2, 4)), dma, dma,
-            dma((2,)), dma, dma, dma, dma((2, NZ - 1)), dma, dma,
-            dma, dma((2, HOPS, 2)), dma, dma,
+            dma((2,)), dma, dma, dma, dma((2, NZ - 1, 2)), dma, dma,
+            dma((2,)), dma((2, HOPS)), dma, dma,
             dma((2,)), dma((2,)), dma((2,)), dma((2,)),
         ],
         compiler_params=pltpu.CompilerParams(
@@ -417,9 +435,8 @@
     attn_proj, expert_sum = pl.pallas_call(
         combine,
         out_shape=(out, out),
-        in_specs=[smem, vmem, vmem, vmem, hbm],
-        out_specs=(hbm, vmem),
-        scratch_shapes=[dma],
+        in_specs=[smem] + [vmem] * 4,
+        out_specs=(vmem, vmem),
     )(capacity[0, 0], ids, gates, tot, proj)
     return (attn_proj[None], expert_sum[None])
 

time: 152 us -> 114 us (0.75)
  the two profiles are of different devices: /device:TPU:25 before, /device:TPU:36 now
where the time goes in v3:
time: 114 us
  Pallas kernels  113 us (99%)
    pallas_call x1, Pallas kernels, body(): pl.pallas_call(kernel, out_shape=(out, jax.ShapeDtypeStruct((2,) + rows,...  110 us
    pallas_call x1, Pallas kernels, body(): pl.pallas_call(combine, out_shape=(out, out), in_specs=[smem] + [vmem] *...  2.58 us

profile of v3, /device:TPU:36, one launch (start us, length us, event | category | flops | bytes accessed | tf_op | source)
XLA Modules:
  0.0 113.6 jit_solution(12745493096310019607)
XLA Ops:
  0.6 110.4 %shard_map.131 = (bf16[128,2048]{1,0:T(8,128)(2,1)}, bf16[2,48,1024]{2,1,0:T(8,128)(2,1)}) custom-call(s32[2]{0:T(128)} %bitcast.27, s32[2]{0:T(128)} %bitcast.25, bf16[128,1024]{1,0:T(8,128)(2,1)} %bitcast.18, bf16[128,1024]{1,0:T(8,128)(2,1)} %bitcast.19, bf16[128,1024]{1,0:T(8,128)(2,1)} %bitcast.20, bf16[128,2048]{1,0:T(8,128)(2,1)} %bitcast.17, ...), custom_call_target="tpu_custom_call" | custom-call | tf_op jit(solution)/shard_map/pallas_call | solution.py:397
  111.0 2.6 %shard_map.132 = (bf16[128,2048]{1,0:T(8,128)(2,1)}, bf16[128,2048]{1,0:T(8,128)(2,1)}) custom-call(s32[2]{0:T(128)} %bitcast.26, s32[6,1,128]{2,1,0:T(1,128)} %bitcast.22, f32[6,1,128]{2,1,0:T(1,128)} %bitcast.24, bf16[2,48,1024]{2,1,0:T(8,128)(2,1)} %get-tuple-element.6.tot_ref, bf16[128,2048]{1,0:T(8,128)(2,1)} %get-tuple-element.7.proj_ref), custom_call_target="tpu_custom_call" | custom-call | tf_op jit(solution)/shard_map/pallas_call | solution.py:435

commit v4 on v3

--- a/solution.py
+++ b/solution.py
@@ -27,8 +27,8 @@
 NT = (((1,), (1,)), ((), ()))
 TN = (((0,), (0,)), ((), ()))
 
-SCHEDULE = "wmwmwmwmmmmwmmmwmwmwmmmwwmwmwmwmwmwmwmwmw"
-GROUPS = ((1, 2, 3, 4), (5, 6, 7, 0))
+SCHEDULE = "mwmwmwmwmwmmmmwmmmwmwmwwmmmwmwmwmwmwmwmwmwm"
+GROUPS = ((1, 2, 5, 6), (3, 0, 7, 4))
 PARTS = ((0, 144), (144, 128))
 
 
@@ -64,10 +64,10 @@
     owner, caps,
     q_ref, k_ref, v_ref, res_ref, wo_ref, wg_ref, wd_ref, gain_ref, ids_ref,
     proj_ref, tot_ref,
-    qkv, abuf, attd, wbuf, res, packed, oth, cand, rsb, xsend, xpiece, wf, uw,
-    normed, rbuf, dsend, sbuf, pbuf,
+    qkv, abuf, attd, wbuf, res, packed, early, lead, oth, cand, rsb, xsend, xpiece, wf, uw,
+    normed, rbuf, dsend, sbuf, a1, b1, sa, sb, a2, b2,
     q_s, q_r, a_s, a_r, z_s, z_r, p1_s, p1_r, p2_s, p2_r, c_s, c_r,
-    l_s, oth_s, oth_r, rs_s, rs_r, xp_s, xp_r, ag_s, ag_r, cc_s, cc_r,
+    l_s, early_s, early_r, oth_s, oth_r, rs_s, rs_r, xp_s, xp_r, ag_s, ag_r, cc_s, cc_r,
     r_s, r_r, e_s, e_r,
 ):
     dp = lax.axis_index("dp")
@@ -93,7 +93,7 @@
     down = at(zz=lax.rem(z + NZ - 1, NZ))
 
     def peer(i):
-        return lax.rem(ctx + i, NCTX)
+        return lax.rem(xh + i // NY, 2) * NY + lax.rem(y + i % NY, NY)
 
     def send(src, dst, ssem, rsem, dev):
         pltpu.make_async_remote_copy(
@@ -108,8 +108,9 @@
         pltpu.make_async_copy(dst, dst, sem).wait()
 
     barrier = pltpu.get_barrier_semaphore()
+    near = (1, 15, 2, 14, 3, 13, 4, 12)
     partners = [sibling]
-    partners += [at(zz=lax.rem(z + i, NZ)) for i in range(1, NZ)]
+    partners += [at(zz=lax.rem(z + i, NZ)) for i in near]
     partners += [(dp, peer(i)) for i in range(1, NCTX)]
     partners += [(line, peer(i)) for i in range(NCTX)]
     for dev in partners:
@@ -122,40 +123,42 @@
     pl.semaphore_wait(barrier, len(partners))
 
     other_rows = pl.ds(pl.multiple_of((1 - core) * HALF_STEP, 16), HALF)
+    firsts = (lax.rem(z + 8, NZ), lax.rem(z + 9, NZ))
+    for d in range(2):
+        send(packed.at[other_rows, cols(firsts[d] * 128, 128)], early.at[d], early_s, early_r, sibling)
     send(packed.at[other_rows, :], oth, oth_s, oth_r, sibling)
     wo_part = wo_ref.at[:, cols(ctx * 256, 256)]
-    for i in range(1, NZ):
-        send(wo_part, wbuf.at[x, y, z, core], z_s, z_r, at(zz=lax.rem(z + i, NZ)))
-    local(wo_part, wbuf.at[x, y, z, core], z_r)
-    for i in range(1, NCTX):
-        for j, ref in enumerate((q_ref, k_ref, v_ref)):
-            send(ref.at[:, cols(peer(i) * HD, HD)], qkv.at[j, ctx], q_s, q_r.at[ctx], (dp, peer(i)))
-    for j, ref in enumerate((q_ref, k_ref, v_ref)):
-        local(ref.at[:, cols(ctx * HD, HD)], qkv.at[j, ctx], q_r.at[ctx])
-
+    for i in near:
+        send(wo_part, wbuf.at[x, y, z, core], z_s.at[0], z_r.at[0], at(zz=lax.rem(z + i, NZ)))
+    local(wo_part, wbuf.at[x, y, z, core], z_r.at[0])
     owners = (owner[0], owner[1])
 
     def weights():
-        arrive(oth, oth_r)
         mate = dp + 1 - 2 * core
         own_rows = pl.ds(pl.multiple_of(core * HALF_STEP, 16), HALF)
-        has = []
-        for e in range(2):
-            mine = owners[e] == dp
-            mates = owners[e] == mate
-            has.append(jnp.logical_or(mine, mates))
-            for c in range(NZ):
-                a = packed[own_rows, c * 128:(c + 1) * 128]
-                b = oth[:, c * 128:(c + 1) * 128]
-                cand[e, c] = lax.select(mine, a, lax.select(mates, b, jnp.zeros_like(b)))
+        mine = [owners[e] == dp for e in range(2)]
+        mates = [owners[e] == mate for e in range(2)]
+        has = [jnp.logical_or(mine[e], mates[e]) for e in range(2)]
+
+        def pick(e, a, b):
+            return lax.select(mine[e], a, lax.select(mates[e], b, jnp.zeros_like(b)))
+
         to = (up, down)
+        arrive(early, early_r)
         for d in range(2):
-            c = lax.rem(z + 8, NZ) if d == 0 else lax.rem(z + 9, NZ)
+            a = packed[own_rows, cols(firsts[d] * 128, 128)]
             for e in range(2):
+                lead[e, d] = pick(e, a, early[d])
                 for h in range(2):
                     dst = rsb.at[e, HOPS * d, span(h)]
-                    send(cand.at[e, c, span(h)], dst, rs_s, rs_r.at[e, HOPS * d, h], to[d])
-        yield
+                    send(lead.at[e, d, span(h)], dst, rs_s, rs_r.at[e, HOPS * d, h], to[d])
+        yield
+        arrive(oth, oth_r)
+        for c in range(NZ):
+            a = packed[own_rows, c * 128:(c + 1) * 128]
+            b = oth[:, c * 128:(c + 1) * 128]
+            for e in range(2):
+                cand[e, c] = pick(e, a, b)
         for t in range(HOPS):
             for d in range(2):
                 last = HOPS - 1 - d
@@ -225,7 +228,21 @@
         return wbuf.at[xx, :, pl.ds(8, 8), core]
 
     def main():
-        arrive(wbuf.at[x, y, :, core], z_r)
+        for i in range(1, NCTX):
+            for j, ref in enumerate((q_ref, k_ref, v_ref)):
+                send(ref.at[:, cols(peer(i) * HD, HD)], qkv.at[j, ctx], q_s, q_r.at[ctx], (dp, peer(i)))
+        for j, ref in enumerate((q_ref, k_ref, v_ref)):
+            local(ref.at[:, cols(ctx * HD, HD)], qkv.at[j, ctx], q_r.at[ctx])
+        yield
+        arrive(wbuf.at[0, 0, pl.ds(0, 9), 0], z_r.at[0])
+        for i in (1, 2, 3, 4):
+            block = wbuf.at[x, y, lax.rem(z + NZ - i, NZ), core]
+            send(block, block, z_s.at[1], z_r.at[1], at(zz=lax.rem(z + 4, NZ)))
+            if i < 4:
+                block = wbuf.at[x, y, lax.rem(z + i, NZ), core]
+                send(block, block, z_s.at[1], z_r.at[1], at(zz=lax.rem(z + 12, NZ)))
+        yield
+        arrive(wbuf.at[0, 0, pl.ds(0, 7), 0], z_r.at[1])
         a_own = wbuf.at[x, y, pl.ds(0, 8), core]
         b_own = wbuf.at[x, y, pl.ds(8, 8), core]
         for i in range(1, 4):
@@ -294,8 +311,8 @@
             rows = dot(first.astype(BF), normed[:, :1024]) + dot(second.astype(BF), normed[:, 1024:])
             dst[...] = rows.astype(BF)
         slot = rbuf.at[xl, ctx]
-        for i in (4, 5, 6, 7, 1, 2, 3, 0):
-            group = 0 if i >= 4 else 1
+        for i in (2, 6, 3, 7, 1, 5, 4, 0):
+            group = 0 if i % NY >= 2 else 1
             if i:
                 send(slot, slot, r_s.at[0], r_r.at[group], (dp, peer(i)))
             send(dsend, slot, r_s.at[1], r_r.at[group], (line, peer(i)))
@@ -330,25 +347,48 @@
         out = jnp.concatenate(halves, axis=1).astype(BF)
         for j, i in enumerate(group):
             for s in range(2):
-                sbuf[s, i] = out[2 * j + s]
-        for i in group:
-            if i:
-                send(sbuf.at[0, i], pbuf.at[xl, ctx], e_s.at[0], e_r.at[0], (dp, peer(i)))
-            send(sbuf.at[1, i], pbuf.at[xl, ctx], e_s.at[1], e_r.at[1], (line, peer(i)))
-
-    arrive(pbuf.at[0, pl.ds(0, 7)], e_r.at[0])
-    acc = sbuf[0, 0].astype(F32)
-    for i in range(1, NCTX):
-        acc += pbuf[xl, peer(i)].astype(F32)
-    tot_ref[xl] = acc.astype(BF)
-    arrive(pbuf.at[0], e_r.at[1])
-    acc = pbuf[1 - xl, 0].astype(F32)
-    for i in range(1, NCTX):
-        acc += pbuf[1 - xl, i].astype(F32)
-    tot_ref[1 - xl] = acc.astype(BF)
-
+                xx = lax.rem(xh + i // NY, 2) * 2 + (xl if s == 0 else 1 - xl)
+                for h in range(2):
+                    sbuf[h, xx, lax.rem(y + i % NY, NY)] = out[2 * j + s, :, h * 512:(h + 1) * 512]
+        for i in ((1, 2), (3,))[g]:
+            yy = lax.rem(y + i, NY)
+            send(sbuf.at[0, :, yy], a1.at[y], e_s.at[0], e_r.at[0], at(yy=yy))
+
+    across = [lax.rem(x + i, NX) for i in range(NX)]
+    along = [lax.rem(y + i, NY) for i in range(NY)]
+    for i in (1, 3, 2):
+        send(sbuf.at[1, across[i]], b1.at[x], e_s.at[1], e_r.at[1], at(xx=across[i]))
+
+    def wide(*parts):
+        acc = parts[0].astype(F32)
+        for part in parts[1:]:
+            acc += part.astype(F32)
+        return acc.astype(BF)
+
+    arrive(a1.at[pl.ds(0, 3)], e_r.at[0])
+    for i in (2, 1, 3, 0):
+        xx = across[i]
+        sa[xx] = wide(sbuf[0, xx, y], *[a1[along[j], xx] for j in range(1, NY)])
+        if i:
+            send(sa.at[xx], a2.at[x], e_s.at[2], e_r.at[2], at(xx=xx))
+    arrive(b1.at[pl.ds(0, 3)], e_r.at[1])
+    for i in (2, 1, 3, 0):
+        yy = along[i]
+        sb[yy, 0] = wide(sbuf[1, x, yy], b1[across[2], yy])
+        sb[yy, 1] = wide(b1[across[1], yy], b1[across[3], yy])
+        if i:
+            send(sb.at[yy], b2.at[y], e_s.at[3], e_r.at[3], at(yy=yy))
+    arrive(a2.at[pl.ds(0, 3)], e_r.at[2])
+    tot_ref[xl, :, :512] = wide(sa[x], a2[across[2]])
+    tot_ref[1 - xl, :, :512] = wide(a2[across[1]], a2[across[3]])
+    arrive(b2.at[pl.ds(0, 3)], e_r.at[3])
+    for s, e in ((0, xl), (1, 1 - xl)):
+        tot_ref[e, :, 512:] = wide(sb[y, s], *[b2[along[j], s] for j in range(1, NY)])
+
+    arrive(early, early_s)
     arrive(oth, oth_s)
-    arrive(wbuf.at[0, 0, pl.ds(0, NZ - 1), 0], z_s)
+    arrive(wbuf.at[0, 0, pl.ds(0, 8), 0], z_s.at[0])
+    arrive(wbuf.at[0, 0, pl.ds(0, 7), 0], z_s.at[1])
     arrive(qkv.at[:, pl.ds(0, NCTX - 1)], q_s)
     arrive(abuf.at[pl.ds(0, NCTX - 1)], a_s)
     arrive(wbuf.at[pl.ds(0, 3), pl.ds(0, 2), pl.ds(0, 8), 0], p1_s)
@@ -359,9 +399,10 @@
     arrive(wf.at[0, :, pl.ds(0, 7 * 128)], ag_s.at[0])
     arrive(wf.at[0, :, pl.ds(0, 8 * 128)], ag_s.at[1])
     arrive(wf.at[0], cc_s)
-    for sems, buf in ((r_s, rbuf), (e_s, pbuf)):
-        arrive(buf.at[0, pl.ds(0, 7)], sems.at[0])
-        arrive(buf.at[0], sems.at[1])
+    arrive(rbuf.at[0, pl.ds(0, 7)], r_s.at[0])
+    arrive(rbuf.at[0], r_s.at[1])
+    for i, buf in enumerate((a1, b1, a2, b2)):
+        arrive(buf.at[pl.ds(0, 3)], e_s.at[i])
 
 
 def combine(caps, ids_ref, gates_ref, tot_ref, proj_ref, out_ref, sum_ref):
@@ -392,6 +433,7 @@
     dma = pltpu.SemaphoreType.DMA
     out = jax.ShapeDtypeStruct((TOK, D), BF)
     rows = (2 * CAP, 1024)
+    half = (2 * CAP, 512)
     ids = jnp.transpose(expert_ids, (2, 0, 1))
     gates = jnp.transpose(route_gates, (2, 0, 1))
     proj, tot = pl.pallas_call(
@@ -406,6 +448,8 @@
             pltpu.VMEM((NX, NY, NZ, 2, 16, 256), BF),
             pltpu.VMEM((TOK, D), BF),
             pltpu.VMEM((3 * FF_DEV, D), BF),
+            pltpu.VMEM((2, HALF, 128), BF),
+            pltpu.VMEM((2, 2, HALF, 128), BF),
             pltpu.VMEM((HALF, D), BF),
             pltpu.VMEM((2, NZ, HALF, 128), BF),
             pltpu.VMEM((2, NZ - 1, HALF, 128), BF),
@@ -416,13 +460,18 @@
             pltpu.VMEM((TOK, D), BF),
             pltpu.VMEM((2, NCTX) + rows, BF),
             pltpu.VMEM(rows, BF),
-            pltpu.VMEM((2, NCTX) + rows, BF),
-            pltpu.VMEM((2, NCTX) + rows, BF),
-            dma, dma((NCTX,)), dma, dma, dma, dma,
+            pltpu.VMEM((2, NX, NY) + half, BF),
+            pltpu.VMEM((NY, NX) + half, BF),
+            pltpu.VMEM((NX, NY) + half, BF),
+            pltpu.VMEM((NX,) + half, BF),
+            pltpu.VMEM((NY, 2) + half, BF),
+            pltpu.VMEM((NX,) + half, BF),
+            pltpu.VMEM((NY, 2) + half, BF),
+            dma, dma((NCTX,)), dma, dma, dma((2,)), dma((2,)),
             dma, dma((2,)), dma, dma((2, 4)), dma, dma,
-            dma((2,)), dma, dma, dma, dma((2, NZ - 1, 2)), dma, dma,
+            dma((2,)), dma, dma, dma, dma, dma, dma((2, NZ - 1, 2)), dma, dma,
             dma((2,)), dma((2, HOPS)), dma, dma,
-            dma((2,)), dma((2,)), dma((2,)), dma((2,)),
+            dma((2,)), dma((2,)), dma((4,)), dma((4,)),
         ],
         compiler_params=pltpu.CompilerParams(
             collective_id=0, has_side_effects=True, vmem_limit_bytes=58 << 20

time: 114 us -> 106 us (0.930)
  the two profiles are of different devices: /device:TPU:36 before, /device:TPU:32 now
where the time goes in v4:
time: 106 us; the launch traced here: 105 us
  Pallas kernels  105 us (99%)
    pallas_call x1, Pallas kernels, body(): pl.pallas_call(kernel, out_shape=(out, jax.ShapeDtypeStruct((2,) + rows,...  102 us
    pallas_call x1, Pallas kernels, body(): pl.pallas_call(combine, out_shape=(out, out), in_specs=[smem] + [vmem] *...  2.57 us

profile of v4, /device:TPU:32, one launch (start us, length us, event | category | flops | bytes accessed | tf_op | source)
XLA Modules:
  0.0 105.3 jit_solution(14707330519923673443)
XLA Ops:
  0.6 102.1 %shard_map.131 = (bf16[128,2048]{1,0:T(8,128)(2,1)}, bf16[2,48,1024]{2,1,0:T(8,128)(2,1)}) custom-call(s32[2]{0:T(128)} %bitcast.27, s32[2]{0:T(128)} %bitcast.25, bf16[128,1024]{1,0:T(8,128)(2,1)} %bitcast.18, bf16[128,1024]{1,0:T(8,128)(2,1)} %bitcast.19, bf16[128,1024]{1,0:T(8,128)(2,1)} %bitcast.20, bf16[128,2048]{1,0:T(8,128)(2,1)} %bitcast.17, ...), custom_call_target="tpu_custom_call" | custom-call | tf_op jit(solution)/shard_map/pallas_call | solution.py:439
  102.8 2.6 %shard_map.132 = (bf16[128,2048]{1,0:T(8,128)(2,1)}, bf16[128,2048]{1,0:T(8,128)(2,1)}) custom-call(s32[2]{0:T(128)} %bitcast.26, s32[6,1,128]{2,1,0:T(1,128)} %bitcast.22, f32[6,1,128]{2,1,0:T(1,128)} %bitcast.24, bf16[2,48,1024]{2,1,0:T(8,128)(2,1)} %get-tuple-element.6.tot_ref, bf16[128,2048]{1,0:T(8,128)(2,1)} %get-tuple-element.7.proj_ref), custom_call_target="tpu_custom_call" | custom-call | tf_op jit(solution)/shard_map/pallas_call | solution.py:484

commit v5 on v4

--- a/solution.py
+++ b/solution.py
@@ -27,7 +27,7 @@
 NT = (((1,), (1,)), ((), ()))
 TN = (((0,), (0,)), ((), ()))
 
-SCHEDULE = "mwmwmwmwmwmmmmwmmmwmwmwwmmmwmwmwmwmwmwmwmwm"
+SCHEDULE = "mwmwmwmwmwmmmmwmmmwmwmwmwmmmwmwmwmwmwmwmwmw"
 GROUPS = ((1, 2, 5, 6), (3, 0, 7, 4))
 PARTS = ((0, 144), (144, 128))
 

time: 106 us -> 103 us (0.972)
  the two profiles are of different devices: /device:TPU:32 before, /device:TPU:25 now
where the time goes in v5:
time: 103 us; the launch traced here: 101 us
  Pallas kernels  100 us (97%)
    pallas_call x1, Pallas kernels, body(): pl.pallas_call(kernel, out_shape=(out, jax.ShapeDtypeStruct((2,) + rows,...  97.7 us
    pallas_call x1, Pallas kernels, body(): pl.pallas_call(combine, out_shape=(out, out), in_specs=[smem] + [vmem] *...  2.57 us

profile of v5, /device:TPU:25, one launch (start us, length us, event | category | flops | bytes accessed | tf_op | source)
XLA Modules:
  0.0 101.0 jit_solution(3378922457766302485)
XLA Ops:
  0.6 97.7 %shard_map.131 = (bf16[128,2048]{1,0:T(8,128)(2,1)}, bf16[2,48,1024]{2,1,0:T(8,128)(2,1)}) custom-call(s32[2]{0:T(128)} %bitcast.27, s32[2]{0:T(128)} %bitcast.25, bf16[128,1024]{1,0:T(8,128)(2,1)} %bitcast.18, bf16[128,1024]{1,0:T(8,128)(2,1)} %bitcast.19, bf16[128,1024]{1,0:T(8,128)(2,1)} %bitcast.20, bf16[128,2048]{1,0:T(8,128)(2,1)} %bitcast.17, ...), custom_call_target="tpu_custom_call" | custom-call | tf_op jit(solution)/shard_map/pallas_call | solution.py:439
  98.4 2.6 %shard_map.132 = (bf16[128,2048]{1,0:T(8,128)(2,1)}, bf16[128,2048]{1,0:T(8,128)(2,1)}) custom-call(s32[2]{0:T(128)} %bitcast.26, s32[6,1,128]{2,1,0:T(1,128)} %bitcast.22, f32[6,1,128]{2,1,0:T(1,128)} %bitcast.24, bf16[2,48,1024]{2,1,0:T(8,128)(2,1)} %get-tuple-element.6.tot_ref, bf16[128,2048]{1,0:T(8,128)(2,1)} %get-tuple-element.7.proj_ref), custom_call_target="tpu_custom_call" | custom-call | tf_op jit(solution)/shard_map/pallas_call | solution.py:484

commit v6 on v5

--- a/solution.py
+++ b/solution.py
@@ -27,7 +27,7 @@
 NT = (((1,), (1,)), ((), ()))
 TN = (((0,), (0,)), ((), ()))
 
-SCHEDULE = "mwmwmwmwmwmmmmwmmmwmwmwmwmmmwmwmwmwmwmwmwmw"
+SCHEDULE = "mwmwmwmwmwmmmmwmmmwmwmwmwmwmmwmwmwmwmwmwmwmw"
 GROUPS = ((1, 2, 5, 6), (3, 0, 7, 4))
 PARTS = ((0, 144), (144, 128))
 
@@ -182,6 +182,7 @@
         known = jnp.where(xl == 0, has[1].astype(jnp.int32), has[0].astype(jnp.int32)) > 0
         xsend[...] = settled(1 - xl, known)
         send(xsend, xpiece, xp_s, xp_r, partner)
+        yield
         known = jnp.where(xl == 0, has[0].astype(jnp.int32), has[1].astype(jnp.int32)) > 0
         here = settled(xl, known)
         arrive(xpiece, xp_r)

time: 103 us -> 104 us (level)
  the two profiles are of different devices: /device:TPU:25 before, /device:TPU:32 now
where the time goes in v6:
time: 104 us; the launch traced here: 103 us
  Pallas kernels  103 us (99%)
    pallas_call x1, Pallas kernels, body(): pl.pallas_call(kernel, out_shape=(out, jax.ShapeDtypeStruct((2,) + rows,...  100 us
    pallas_call x1, Pallas kernels, body(): pl.pallas_call(combine, out_shape=(out, out), in_specs=[smem] + [vmem] *...  2.57 us

profile of v6, /device:TPU:32, one launch (start us, length us, event | category | flops | bytes accessed | tf_op | source)
XLA Modules:
  0.0 103.4 jit_solution(10322378476768621704)
XLA Ops:
  0.6 100.2 %shard_map.131 = (bf16[128,2048]{1,0:T(8,128)(2,1)}, bf16[2,48,1024]{2,1,0:T(8,128)(2,1)}) custom-call(s32[2]{0:T(128)} %bitcast.27, s32[2]{0:T(128)} %bitcast.25, bf16[128,1024]{1,0:T(8,128)(2,1)} %bitcast.18, bf16[128,1024]{1,0:T(8,128)(2,1)} %bitcast.19, bf16[128,1024]{1,0:T(8,128)(2,1)} %bitcast.20, bf16[128,2048]{1,0:T(8,128)(2,1)} %bitcast.17, ...), custom_call_target="tpu_custom_call" | custom-call | tf_op jit(solution)/shard_map/pallas_call | solution.py:440
  100.8 2.6 %shard_map.132 = (bf16[128,2048]{1,0:T(8,128)(2,1)}, bf16[128,2048]{1,0:T(8,128)(2,1)}) custom-call(s32[2]{0:T(128)} %bitcast.26, s32[6,1,128]{2,1,0:T(1,128)} %bitcast.22, f32[6,1,128]{2,1,0:T(1,128)} %bitcast.24, bf16[2,48,1024]{2,1,0:T(8,128)(2,1)} %get-tuple-element.6.tot_ref, bf16[128,2048]{1,0:T(8,128)(2,1)} %get-tuple-element.7.proj_ref), custom_call_target="tpu_custom_call" | custom-call | tf_op jit(solution)/shard_map/pallas_call | solution.py:485
